TPU v7x, 32 devices: a whole 2x2x4 slice. The times are simulated.
32 devices in a mesh: ctx: 8 (over z, y), head: 4 (over x, core).
Axes of the slice: x: 2, y: 2, z: 4, core: 2. Of those that a mesh axis runs over, the one named last changes fastest.
Arguments:
- x_in: bfloat16 [4096, 8192], P('ctx', 'head'), may hold values from -6 to 6
- z_in: bfloat16 [4096, 8192], P('ctx', 'head'), may hold values from -6 to 6
- bc_in: bfloat16 [4096, 256], P('ctx', 'head'), may hold values from -6 to 6
- dt: float32 [4096, 128], P('ctx', 'head'), may hold values from 4.8828125e-05 to 0.25146484, as said below
- decay_scale: float32 [128], P('head'), may hold values from 0.5 to 2
- conv_x: bfloat16 [4, 8192], P(None, 'head'), may hold values from -3 to 3
- conv_bc: bfloat16 [4, 256], P(None, 'head'), may hold values from -3 to 3
- norm_gain: bfloat16 [8192], P('head'), may hold values from 0.25 to 1.75
- doc_start: int32 [4096], P('ctx'), may hold values from 0 to 1, as said below
Outputs:
- out: bfloat16 [4096, 8192], P('ctx', 'head')
Inputs may be any that keep to these rules, and one draw needn't show every extreme that they name: doc_start[0] = 0; going round the loop, two consecutive ones are at most 512 apart; the document that holds position 0 is exactly 512 long and begins 3 (4 - 1) or more positions before the end. `dt`: positive step sizes.
All inputs are finite; a program needn't handle non-finite values.
Results may differ from a plain program's by a relative error of at most 0.0034.
Values may be sent and summed in bfloat16 or wider, within the bound.
No kernel may reach another device: no remote copies, remote signals or barrier semaphores. Data moves between devices by JAX's collectives and lax.ppermute only.
A program may use at most 64 MiB of HBM per device.

v0:
```python
import jax
import jax.numpy as jnp
from jax import lax
from jax.sharding import PartitionSpec as P

HDIM = 64
DSTATE = 128
BLOCK = 256
CONV = 4


def shifted(value, axis, steps):
    count = lax.axis_size(axis)
    pairs = [(source, (source + steps) % count) for source in range(count)]
    return lax.ppermute(value, axis, pairs)


def causal_conv(padded, taps, same):
    rows = same.shape[1]
    total = jnp.zeros((rows, taps.shape[1]), jnp.float32)
    for offset in range(taps.shape[0]):
        piece = padded[offset : offset + rows].astype(jnp.float32) * taps[offset].astype(
            jnp.float32
        )
        total = total + jnp.where(same[offset][:, None], piece, 0.0)
    return jax.nn.silu(total)


def block_pass(state, values, bmat, cmat, steps, scale, doc_ids, doc_before):
    high = lax.Precision.HIGHEST
    log_decay = jnp.cumsum(-steps * scale[None, :], axis=0)
    scores = jnp.dot(cmat, bmat.T, precision=high)
    rows = doc_ids.shape[0]
    lower = jnp.arange(rows)[:, None] >= jnp.arange(rows)[None, :]
    keep = lower & (doc_ids[:, None] == doc_ids[None, :])
    decay_t = log_decay.T
    spread = decay_t[:, :, None] - decay_t[:, None, :]
    weights = (
        jnp.where(keep[None, :, :], jnp.exp(jnp.minimum(spread, 0.0)), 0.0) * scores[None, :, :]
    )
    output = jnp.einsum("hts,shp->htp", weights, values, precision=high)
    live = doc_ids == doc_before
    carried = jnp.einsum("tn,hpn->htp", cmat, state, precision=high)
    output = output + jnp.where(live[None, :, None], jnp.exp(decay_t)[:, :, None] * carried, 0.0)
    tail = doc_ids == doc_ids[-1]
    to_end = jnp.where(tail[:, None], jnp.exp(log_decay[-1][None, :] - log_decay), 0.0)
    fresh = jnp.einsum("sh,shp,sn->hpn", to_end, values, bmat, precision=high)
    keep_state = jnp.where(doc_ids[-1] == doc_before, jnp.exp(log_decay[-1]), 0.0)
    return (keep_state[:, None, None] * state + fresh, output)


def gated_norm(output, gate, gain):
    rows, heads, width = output.shape
    mixed = output * jax.nn.silu(gate.astype(jnp.float32)).reshape(rows, heads, width)
    factor = lax.rsqrt(jnp.mean(mixed * mixed, axis=-1, keepdims=True) + 1e-05)
    normed = mixed * factor * gain.astype(jnp.float32).reshape(heads, width)
    return normed.reshape(rows, heads * width).astype(jnp.bfloat16)


def on_device(x_in, z_in, bc_in, dt, decay_scale, conv_x, conv_bc, norm_gain, doc_start):
    high = lax.Precision.HIGHEST
    positions = x_in.shape[0]
    local_heads = dt.shape[1]
    lead = CONV - 1
    doc_ids = jnp.cumsum(doc_start)
    in_last = (doc_ids[-lead:] == doc_ids[-1])[:, None]
    tail_x = jnp.where(in_last, x_in[-lead:], jnp.zeros_like(x_in[-lead:]))
    tail_bc = jnp.where(in_last, bc_in[-lead:], jnp.zeros_like(bc_in[-lead:]))
    rim_x, rim_bc = shifted((tail_x, tail_bc), "ctx", 1)
    x_pad = jnp.concatenate([rim_x, x_in], axis=0)
    bc_pad = jnp.concatenate([rim_bc, bc_in], axis=0)
    ids_pad = jnp.concatenate([jnp.zeros((lead,), jnp.int32), doc_ids], axis=0)
    same = jnp.stack([ids_pad[offset : offset + positions] == doc_ids for offset in range(CONV)])
    x_conv = causal_conv(x_pad, conv_x, same)
    bc_local = causal_conv(bc_pad, conv_bc, same).astype(jnp.bfloat16)
    bc_whole = lax.all_gather(bc_local, "head", axis=1, tiled=True).astype(jnp.float32)
    bmat = bc_whole[:, :DSTATE]
    cmat = bc_whole[:, DSTATE:]
    blocks = positions // BLOCK
    empty = jnp.zeros((local_heads, HDIM, DSTATE), jnp.float32)
    end_state = empty
    pieces = []
    for index in range(blocks):
        low = index * BLOCK
        high_end = low + BLOCK
        before = jnp.full((), -1, jnp.int32) if index == 0 else doc_ids[low - 1]
        block_values = x_conv[low:high_end].reshape(BLOCK, local_heads, HDIM)
        end_state, block_out = block_pass(
            end_state,
            block_values,
            bmat[low:high_end],
            cmat[low:high_end],
            dt[low:high_end],
            decay_scale,
            doc_ids[low:high_end],
            before,
        )
        pieces.append(block_out)
    output = jnp.concatenate(pieces, axis=1)
    device_decay = jnp.cumsum(-dt * decay_scale[None, :], axis=0)
    through = jnp.where(doc_ids[-1] == 0, jnp.exp(device_decay[-1]), 0.0)

    def relay_turn(turn, incoming):
        return shifted(through[:, None, None] * incoming + end_state, "ctx", 1)

    state_in = lax.fori_loop(0, lax.axis_size("ctx") // 8, relay_turn, empty)
    carried = jnp.einsum("tn,hpn->htp", cmat, state_in, precision=high)
    live = (doc_ids == 0)[None, :, None]
    output = output + jnp.where(live, jnp.exp(device_decay.T)[:, :, None] * carried, 0.0)
    return gated_norm(jnp.transpose(output, (1, 0, 2)), z_in, norm_gain)


def solution(mesh):
    in_specs = (
        P("ctx", "head"),
        P("ctx", "head"),
        P("ctx", "head"),
        P("ctx", "head"),
        P("head"),
        P(None, "head"),
        P(None, "head"),
        P("head"),
        P("ctx"),
    )
    out_specs = P("ctx", "head")
    return jax.shard_map(
        on_device, mesh=mesh, in_specs=in_specs, out_specs=out_specs, check_vma=False
    )
```

profile of v0, /device:TPU:0, one launch (start us, length us, event | category | flops | bytes accessed | tf_op | source)
XLA Modules:
  0.0 98.0 jit_solution(13949360632276049648)
XLA Ops:
  0.0 1.0 %reduce-window.29 = s32[4,128]{1,0:T(4,128)S(1)} reduce-window(s32[4,128]{1,0:T(4,128)} %bitcast.145, s32[]{:T(128)} %constant.12.clone.1), window={size=1x128 pad=0_0x127_0}, to_apply=%region_0.0 | reduce-window | flops 65024 | bytes 4100 | tf_op jit(solution)/shard_map/reduce-window
  1.0 0.1 slice.151
  1.1 0.1 slice_reduce_fusion.5
  1.2 0.6 broadcast_compare_fusion
  1.8 0.6 fusion.84
  2.4 0.7 slice_compare_fusion
  3.1 0.8 slice_select_fusion.1
  3.9 3.0 %collective-permute-start = (bf16[3,64]{0,1:T(8,128)(2,1)S(1)}, bf16[3,64]{0,1:T(8,128)(2,1)S(1)}, u32[]{:S(2)}, u32[]{:S(2)}) collective-permute-start(bf16[3,64]{0,1:T(8,128)(2,1)S(1)} %slice_select_fusion.1), channel_id=1, source_target_pairs={{0,4},{4,8},{8,12},{12,16},{16,20},{20,24},{24,28},{28,0},{1,5},{5... | collective-permute-start | bytes 1160 | tf_op jit(solution)/shard_map/ppermute | solution.py:15
  6.9 0.8 slice_select_fusion
  7.7 1.6 %collective-permute-start.1 = (bf16[3,2048]{1,0:T(4,128)(2,1)S(1)}, bf16[3,2048]{1,0:T(4,128)(2,1)S(1)}, u32[]{:S(2)}, u32[]{:S(2)}) collective-permute-start(bf16[3,2048]{1,0:T(4,128)(2,1)S(1)} %slice_select_fusion), channel_id=1, source_target_pairs={{0,4},{4,8},{8,12},{12,16},{16,20},{20,24},{24,28},{28,0},{1,5},{5... | collective-permute-start | bytes 36872 | tf_op jit(solution)/shard_map/ppermute | solution.py:15
  9.3 0.1 fusion.72
  9.4 0.7 slice.189
  10.0 0.6 slice.194
  10.6 0.8 fusion.50
  11.4 0.8 multiply_bitcast_fusion.1
  12.3 0.6 reduce-window.35
  12.9 0.2 slice_reduce_fusion.1
  13.1 0.7 fusion.82
  13.8 0.7 fusion.81
  15.1 0.9 copy_bitcast_fusion
  16.0 0.6 reduce-window.31
  16.6 0.2 slice_reduce_fusion.2
  16.8 0.7 copy_bitcast_fusion.2
  17.5 0.7 fusion.79
  18.1 1.1 %reduce-window.39 = f32[32,4,128]{2,0,1:T(8,128)S(1)} reduce-window(f32[32,4,128]{2,0,1:T(8,128)S(1)} %copy_bitcast_fusion, f32[]{:T(128)} %constant.13.clone.1), window={size=1x1x128 pad=0_0x0_0x127_0}, to_apply=%region_6.7 | reduce-window | flops 2080768 | bytes 131076 | tf_op jit(solution)/shard_map/reduce-window.6
  19.3 0.2 slice_reduce_fusion
  19.5 0.1 bitcast_bitcast_fusion
  19.6 0.1 bitcast_exponential_fusion
  19.7 0.8 bitcast_convert_fusion.3
  21.7 2.5 %broadcast_compare_fusion.1 = (pred[256]{0:T(512)(128)(4,1)S(1)}, pred[256]{0:T(512)(128)(4,1)}, pred[256]{0:T(512)(128)(4,1)S(1)}, pred[256]{0:T(512)(128)(4,1)}) fusion(s32[]{:T(128)} %bitcast.27, s32[4,128]{1,0:T(4,128)S(1)} %get-tuple-element.16, s32[]{:T(128)} %bitcast.19, s32[]{:T(128)} %bitcast.20), kind=kLoop, calls=%fused_computation.127 | loop fusion | flops 1024 | bytes 3084 | tf_op jit(solution)/shard_map/eq | solution.py:45
  24.2 0.2 slice_reduce_fusion.4
  24.4 0.9 slice_convert_fusion.3
  26.0 0.1 exponential_select_fusion.1
  26.1 0.5 fusion.75
  26.6 0.2 slice_reduce_fusion.3
  26.8 0.1 exponential_select_fusion
  26.9 0.5 broadcast_select_fusion
  27.4 4.7 %convert_multiply_fusion = f32[512,2048]{1,0:T(8,128)} fusion(bf16[512,2048]{1,0:T(8,128)(2,1)} %param.10), kind=kLoop, calls=%fused_computation.12 | loop fusion | flops 5242880 | bytes 6291456 | tf_op jit(solution)/shard_map/jit(silu)/mul | solution.py:54
  32.0 0.8 fusion.71
  32.8 5.5 %copy.68 = f32[512,2048]{0,1:T(8,128)} copy(f32[512,2048]{1,0:T(8,128)} %convert_multiply_fusion) | data formatting | bytes 8388608 | tf_op jit(solution)/shard_map/jit(silu)/mul | solution.py:54
  38.3 0.0 copy-done.15
  38.3 0.1 reshape.296
  38.4 0.0 collective-permute-done
  38.4 0.2 multiply_convert_fusion.1
  38.6 5.8 %all_gather.3 = bf16[512,256]{0,1:T(8,128)(2,1)S(1)} all-gather(bf16[512,64]{0,1:T(8,128)(2,1)S(1)} %multiply_convert_fusion.1), channel_id=1, replica_groups=mesh['ctx'=8,'head'=4] {'head'}, dimensions={1}, use_global_device_ids=true | all-gather | bytes 327680 | tf_op jit(solution)/shard_map/all_gather | solution.py:76
  44.4 0.9 fusion.59
  45.3 2.3 %fusion.48 = f32[32,64,256]{2,1,0:T(8,128)} fusion(bf16[512,256]{0,1:T(8,128)(2,1)S(1)} %all_gather.3), kind=kOutput, calls=%fused_computation.49 | convolution fusion | flops 805306368 | bytes 2162688 | tf_op jit(solution)/shard_map/tn,hpn->htp/dot_general | solution.py:43
  47.6 0.9 fusion.64
  48.5 0.0 collective-permute-done.1
  48.5 4.2 %divide_multiply_fusion = f32[512,2048]{1,0:T(8,128)S(1)} fusion(bf16[512,2048]{1,0:T(8,128)(2,1)S(1)} %copy-done.3, bf16[3,2048]{1,0:T(4,128)(2,1)S(1)} %collective-permute-done.1, f32[2048]{0:T(1024)S(1)} %bitcast.143, f32[2048]{0:T(1024)S(1)} %bitcast.144, f32[2048]{0:T(1024)S(1)} %bitcast.142, f32[2048]{0:T(1024)S(1)} %bitcast.141, ...), kind=kLoop, calls=%fused_computation.25 | loop fusion | flops 28311552 | bytes 6338048 | tf_op jit(solution)/shard_map/jit(silu)/mul | solution.py:26
  52.7 2.3 %fusion.83 = (f32[256,2048]{1,0:T(8,128)}, f32[256,2048]{1,0:T(8,128)}) fusion(f32[512,2048]{1,0:T(8,128)S(1)} %divide_multiply_fusion), kind=kLoop, calls=%fused_computation.139 | loop fusion | bytes 8388608 | tf_op jit(solution)/shard_map/slice | solution.py:87
  55.0 1.9 %copy.59 = f32[256,2048]{0,1:T(8,128)S(1)} copy(f32[256,2048]{1,0:T(8,128)} %get-tuple-element.20) | data formatting | bytes 4194304 | tf_op jit(solution)/shard_map/slice | solution.py:87
  56.9 1.7 %fusion.37 = f32[32,64,128]{2,1,0:T(8,128)S(1)} fusion(f32[256,32,64]{0,2,1:T(8,128)S(1)} %bitcast.136, f32[256,32]{0,1:T(8,128)S(1)} %exponential_select_fusion.1, f32[32]{0:T(128)} %fusion.75, bf16[512,256]{0,1:T(8,128)(2,1)S(1)} %all_gather.3), kind=kOutput, calls=%fused_computation.44 | convolution fusion | flops 806092800 | bytes 3244160 | tf_op jit(solution)/shard_map/sh,shp,sn->hpn/dot_general | solution.py:47
  58.7 2.4 %fusion.55 = f32[32,64,256]{2,1,0:T(8,128)} fusion(f32[32,64,128]{2,1,0:T(8,128)S(1)} %fusion.37, bf16[512,256]{0,1:T(8,128)(2,1)S(1)} %all_gather.3), kind=kOutput, calls=%fused_computation.68 | convolution fusion | flops 805306368 | bytes 3211264 | tf_op jit(solution)/shard_map/tn,hpn->htp/dot_general | solution.py:43
  61.0 0.0 copy-done.1
  61.0 1.9 %copy.64 = f32[256,2048]{0,1:T(8,128)S(1)} copy(f32[256,2048]{1,0:T(8,128)} %get-tuple-element.18) | data formatting | bytes 4194304 | tf_op jit(solution)/shard_map/slice | solution.py:87
  63.0 1.1 %fusion.43 = f32[32,64,128]{2,1,0:T(8,128)S(1)} fusion(f32[256,32,64]{0,2,1:T(8,128)S(1)} %bitcast.134, f32[256,32]{0,1:T(8,128)S(1)} %exponential_select_fusion, f32[32,64,128]{2,1,0:T(8,128)S(1)} %fusion.37, f32[32]{0:T(128)S(1)} %copy-done.18, f32[32]{0:T(128)S(1)} %copy-done.17, bf16[512,256]{0,1:T(8,128)(2,1)S(1)} %all_gather.3), kind=kOutput, calls=%fused_computation.46 | convolution fusion | flops 806617088 | bytes 4293632 | tf_op jit(solution)/shard_map/sh,shp,sn->hpn/dot_general | solution.py:47
  64.2 1.8 %collective-permute-start.2 = (f32[32,64,128]{2,1,0:T(8,128)S(1)}, f32[32,64,128]{2,1,0:T(8,128)S(1)}, u32[]{:S(2)}, u32[]{:S(2)}) collective-permute-start(f32[32,64,128]{2,1,0:T(8,128)S(1)} %fusion.43), channel_id=1, source_target_pairs={{0,4},{4,8},{8,12},{12,16},{16,20},{20,24},{24,28},{28,0},{1,5},{5... | collective-permute-start | bytes 3145736 | tf_op jit(solution)/shard_map/while/body/eval_jaxpr/ppermute | solution.py:15
  66.0 10.0 %bitcast_add_fusion = f32[32,256,64]{1,2,0:T(8,128)S(1)} fusion(f32[32,64,256]{2,1,0:T(8,128)S(1)} %copy-done.5, f32[256,32,64]{0,2,1:T(8,128)S(1)} %bitcast.135, f32[256,256]{1,0:T(8,128)S(1)} %copy-done.7, f32[32,256]{1,0:T(8,128)S(1)} %copy-done.11, pred[256,256]{1,0:T(8,128)(4,1)S(1)} %copy-done.10, f32[32,256]{1,0:T(8,128)S(1)} %copy-done.13, ...), kind=kOutput, calls=%fused_computation.38 | convolution fusion | flops 1620574208 | bytes 6684928 | tf_op jit(solution)/shard_map/hts,shp->htp/dot_general | solution.py:41
  76.1 10.2 %bitcast_add_fusion.1 = f32[32,256,64]{1,2,0:T(8,128)S(1)} fusion(f32[32,64,256]{2,1,0:T(8,128)S(1)} %copy-done.4, f32[256,32,64]{0,2,1:T(8,128)S(1)} %bitcast.137, f32[256,256]{1,0:T(8,128)S(1)} %copy-done.6, f32[32,256]{1,0:T(8,128)S(1)} %copy-done.12, pred[256,256]{1,0:T(8,128)(4,1)S(1)} %copy-done.9, f32[32,256]{1,0:T(8,128)S(1)} %copy-done.14, ...), kind=kOutput, calls=%fused_computation.39 | convolution fusion | flops 1620574208 | bytes 6684928 | tf_op jit(solution)/shard_map/hts,shp->htp/dot_general | solution.py:41
  86.3 6.2 %collective-permute-done.2 = f32[32,64,128]{2,1,0:T(8,128)S(1)} collective-permute-done((f32[32,64,128]{2,1,0:T(8,128)S(1)}, f32[32,64,128]{2,1,0:T(8,128)S(1)}, u32[]{:S(2)}, u32[]{:S(2)}) %collective-permute-start.2) | collective-permute-done | bytes 1048608 | tf_op jit(solution)/shard_map/while/body/eval_jaxpr/ppermute | solution.py:15
  92.5 2.5 %multiply_reduce_fusion = (f32[512,32]{0,1:T(8,128)S(1)}, f32[512,32,64]{0,2,1:T(8,128)S(1)}) fusion(f32[512,32,64]{0,2,1:T(8,128)S(1)} %bitcast.132, f32[32,64,128]{2,1,0:T(8,128)S(1)} %collective-permute-done.2, bf16[512,256]{0,1:T(8,128)(2,1)S(1)} %all_gather.3, f32[32,512]{1,0:T(8,128)S(1)} %bitcast_exponential_fusion, ...), kind=kOutput, calls=%fused_computation.21 | convolution fusion | flops 1617936384 | bytes 13894144 | tf_op jit(solution)/shard_map/tn,hpn->htp/dot_general | solution.py:107
  95.1 0.5 multiply_convert_fusion
  95.6 2.4 %copy.69 = bf16[512,2048]{1,0:T(8,128)(2,1)} copy(bf16[512,2048]{0,1:T(8,128)(2,1)S(1)} %bitcast.133) | data formatting | bytes 4194304 | tf_op jit(solution)/shard_map/convert_element_type | solution.py:57
  (50 shorter events, 0.3 us)
Async XLA Ops:
  3.9 34.5 %collective-permute-start = (bf16[3,64]{0,1:T(8,128)(2,1)S(1)}, bf16[3,64]{0,1:T(8,128)(2,1)S(1)}, u32[]{:S(2)}, u32[]{:S(2)}) collective-permute-start(bf16[3,64]{0,1:T(8,128)(2,1)S(1)} %slice_select_fusion.1), channel_id=1, source_target_pairs={{0,4},{4,8},{8,12},{12,16},{16,20},{20,24},{24,28},{28,0},{1,5},{5... | collective-permute-start | bytes 1160 | tf_op jit(solution)/shard_map/ppermute | solution.py:15
  7.7 40.8 %collective-permute-start.1 = (bf16[3,2048]{1,0:T(4,128)(2,1)S(1)}, bf16[3,2048]{1,0:T(4,128)(2,1)S(1)}, u32[]{:S(2)}, u32[]{:S(2)}) collective-permute-start(bf16[3,2048]{1,0:T(4,128)(2,1)S(1)} %slice_select_fusion), channel_id=1, source_target_pairs={{0,4},{4,8},{8,12},{12,16},{16,20},{20,24},{24,28},{28,0},{1,5},{5... | collective-permute-start | bytes 36872 | tf_op jit(solution)/shard_map/ppermute | solution.py:15
  32.8 5.5 %copy-start.15 = (bf16[2048]{0:T(1024)(128)(2,1)S(1)}, bf16[2048]{0:T(1024)(128)(2,1)}, u32[]{:S(2)}) copy-start(bf16[2048]{0:T(1024)(128)(2,1)} %param.16) | copy-start | bytes 12292
  32.8 5.6 %copy-start.8 = (bf16[512,64]{0,1:T(8,128)(2,1)S(1)}, bf16[512,64]{0,1:T(8,128)(2,1)}, u32[]{:S(2)}) copy-start(bf16[512,64]{0,1:T(8,128)(2,1)} %param.11) | copy-start | bytes 196612
  32.8 15.7 %copy-start.3 = (bf16[512,2048]{1,0:T(8,128)(2,1)S(1)}, bf16[512,2048]{1,0:T(8,128)(2,1)}, u32[]{:S(2)}) copy-start(bf16[512,2048]{1,0:T(8,128)(2,1)} %param.9) | copy-start | bytes 6291460
  56.9 4.1 %copy-start.1 = (f32[256,2048]{0,1:T(8,128)}, f32[256,2048]{0,1:T(8,128)S(1)}, u32[]{:S(2)}) copy-start(f32[256,2048]{0,1:T(8,128)S(1)} %copy.59) | copy-start | bytes 6291460
  58.6 4.4 %copy-start.17 = (f32[32]{0:T(128)S(1)}, f32[32]{0:T(128)}, u32[]{:S(2)}) copy-start(f32[32]{0:T(128)} %fusion.71) | copy-start | bytes 388
  58.7 4.4 %copy-start.18 = (f32[32]{0:T(128)S(1)}, f32[32]{0:T(128)}, u32[]{:S(2)}) copy-start(f32[32]{0:T(128)} %broadcast_select_fusion) | copy-start | bytes 388
  63.0 3.0 %copy-start.5 = (f32[32,64,256]{2,1,0:T(8,128)S(1)}, f32[32,64,256]{2,1,0:T(8,128)}, u32[]{:S(2)}) copy-start(f32[32,64,256]{2,1,0:T(8,128)} %fusion.55) | copy-start | bytes 6291460
  63.0 3.0 %copy-start.7 = (f32[256,256]{1,0:T(8,128)S(1)}, f32[256,256]{1,0:T(8,128)}, u32[]{:S(2)}) copy-start(f32[256,256]{1,0:T(8,128)} %fusion.59) | copy-start | bytes 786436
  63.0 2.9 %copy-start.10 = (pred[256,256]{1,0:T(8,128)(4,1)S(1)}, pred[256,256]{1,0:T(8,128)(4,1)}, u32[]{:S(2)}) copy-start(pred[256,256]{1,0:T(8,128)(4,1)} %get-tuple-element.50) | copy-start | bytes 196612
  63.0 2.9 %copy-start.11 = (f32[32,256]{1,0:T(8,128)S(1)}, f32[32,256]{1,0:T(8,128)}, u32[]{:S(2)}) copy-start(f32[32,256]{1,0:T(8,128)} %get-tuple-element.24) | copy-start | bytes 98308
  63.0 2.9 %copy-start.13 = (f32[32,256]{1,0:T(8,128)S(1)}, f32[32,256]{1,0:T(8,128)}, u32[]{:S(2)}) copy-start(f32[32,256]{1,0:T(8,128)} %fusion.81) | copy-start | bytes 98308
  63.0 2.9 %copy-start.20 = (pred[256]{0:T(512)(128)(4,1)S(1)}, pred[256]{0:T(512)(128)(4,1)}, u32[]{:S(2)}) copy-start(pred[256]{0:T(512)(128)(4,1)} %get-tuple-element.32) | copy-start | bytes 772
  64.2 28.3 %collective-permute-start.2 = (f32[32,64,128]{2,1,0:T(8,128)S(1)}, f32[32,64,128]{2,1,0:T(8,128)S(1)}, u32[]{:S(2)}, u32[]{:S(2)}) collective-permute-start(f32[32,64,128]{2,1,0:T(8,128)S(1)} %fusion.43), channel_id=1, source_target_pairs={{0,4},{4,8},{8,12},{12,16},{16,20},{20,24},{24,28},{28,0},{1,5},{5... | collective-permute-start | bytes 3145736 | tf_op jit(solution)/shard_map/while/body/eval_jaxpr/ppermute | solution.py:15
  66.0 10.0 %copy-start.2 = (f32[256,2048]{0,1:T(8,128)S(1)}, f32[256,2048]{0,1:T(8,128)}, u32[]{:S(2)}) copy-start(f32[256,2048]{0,1:T(8,128)} %copy-done.1) | copy-start | bytes 6291460
  66.0 10.0 %copy-start.4 = (f32[32,64,256]{2,1,0:T(8,128)S(1)}, f32[32,64,256]{2,1,0:T(8,128)}, u32[]{:S(2)}) copy-start(f32[32,64,256]{2,1,0:T(8,128)} %fusion.48) | copy-start | bytes 6291460
  66.0 10.0 %copy-start.6 = (f32[256,256]{1,0:T(8,128)S(1)}, f32[256,256]{1,0:T(8,128)}, u32[]{:S(2)}) copy-start(f32[256,256]{1,0:T(8,128)} %fusion.64) | copy-start | bytes 786436
  66.0 10.0 %copy-start.9 = (pred[256,256]{1,0:T(8,128)(4,1)S(1)}, pred[256,256]{1,0:T(8,128)(4,1)}, u32[]{:S(2)}) copy-start(pred[256,256]{1,0:T(8,128)(4,1)} %get-tuple-element.51) | copy-start | bytes 196612
  66.0 10.0 %copy-start.12 = (f32[32,256]{1,0:T(8,128)S(1)}, f32[32,256]{1,0:T(8,128)}, u32[]{:S(2)}) copy-start(f32[32,256]{1,0:T(8,128)} %get-tuple-element.25) | copy-start | bytes 98308
  66.0 10.0 %copy-start.14 = (f32[32,256]{1,0:T(8,128)S(1)}, f32[32,256]{1,0:T(8,128)}, u32[]{:S(2)}) copy-start(f32[32,256]{1,0:T(8,128)} %fusion.79) | copy-start | bytes 98308
  66.0 10.0 %copy-start.19 = (pred[256]{0:T(512)(128)(4,1)S(1)}, pred[256]{0:T(512)(128)(4,1)}, u32[]{:S(2)}) copy-start(pred[256]{0:T(512)(128)(4,1)} %get-tuple-element.34) | copy-start | bytes 772
  76.1 16.5 %copy-start = (f32[512,2048]{0,1:T(8,128)S(1)}, f32[512,2048]{0,1:T(8,128)}, u32[]{:S(2)}) copy-start(f32[512,2048]{0,1:T(8,128)} %copy.68) | copy-start | bytes 12582916
  76.1 16.5 %copy-start.16 = (pred[512]{0:T(512)(128)(4,1)S(1)}, pred[512]{0:T(512)(128)(4,1)}, u32[]{:S(2)}) copy-start(pred[512]{0:T(512)(128)(4,1)} %get-tuple-element.11) | copy-start | bytes 1540
where the time goes:
time: 98.6 us; the launch traced here: 98 us
  matrix products  32 us (32%)
  other arithmetic  27.6 us (28%)
  local copies, waits for them, and re-layouts  17.1 us (17%)
  starting transfers between devices  6.29 us (6%)
  waiting for transfers between devices  6.22 us (6%)
  blocking collectives  5.79 us (6%)
  between operations  2.89 us (3%)
    dot_general x2, matrix products, block_pass(): output = jnp.einsum('hts,shp->htp', weights, values, precision=high)  20.2 us
    ppermute x3, starting transfers between devices, shifted(): return lax.ppermute(value, axis, pairs)  6.29 us
    ppermute x3, waiting for transfers between devices, shifted(): return lax.ppermute(value, axis, pairs)  6.22 us
    slice x3, local copies, waits for them, and re-layouts, on_device(): block_values = x_conv[low:high_end].reshape(BLOCK, local_heads, HDIM)  6.14 us
    another operation x12, other arithmetic  5.84 us
    all_gather x1, blocking collectives, on_device(): lax.all_gather(bc_local, 'head', axis=1, tiled=True).astype(jnp.float32)  5.79 us
    mul x1, local copies, waits for them, and re-layouts, gated_norm(): jax.nn.silu(gate.astype(jnp.float32)).reshape(rows, heads, width)  5.5 us
    dot_general x2, matrix products, block_pass(): carried = jnp.einsum('tn,hpn->htp', cmat, state, precision=high)  4.66 us
  transfers between devices with their start and end apart: 3, of which 1 were waited for; matrix products, arithmetic and copies ran while one was open for 53% of the time, Pallas kernels for 0%

commit v1 on v0

--- a/solution.py
+++ b/solution.py
@@ -7,6 +7,18 @@
 DSTATE = 128
 BLOCK = 256
 CONV = 4
+
+
+def _process_boxes(where_dim, field):
+    odd, main = (lax.axis_size("head"), lax.axis_index("head"))
+    b_next, shaped = (field, 1)
+    while shaped < odd:
+        carry_out = lax.ppermute(b_next, "head", [(d, d ^ shaped) for d in range(odd)])
+        view_out = jnp.concatenate([b_next, carry_out], axis=where_dim)
+        b_now = jnp.concatenate([carry_out, b_next], axis=where_dim)
+        b_next = jnp.where(main & shaped == 0, view_out, b_now)
+        shaped = 2 * shaped
+    return b_next
 
 
 def shifted(value, axis, steps):
@@ -73,7 +85,7 @@
     same = jnp.stack([ids_pad[offset : offset + positions] == doc_ids for offset in range(CONV)])
     x_conv = causal_conv(x_pad, conv_x, same)
     bc_local = causal_conv(bc_pad, conv_bc, same).astype(jnp.bfloat16)
-    bc_whole = lax.all_gather(bc_local, "head", axis=1, tiled=True).astype(jnp.float32)
+    bc_whole = _process_boxes(1, bc_local).astype(jnp.float32)
     bmat = bc_whole[:, :DSTATE]
     cmat = bc_whole[:, DSTATE:]
     blocks = positions // BLOCK

time: 98.6 us -> 84.3 us (0.85)
  other arithmetic: 27.6 us -> 21.6 us
  blocking collectives: 5.79 us -> 0 us
  matrix products: 32 us -> 28.9 us
  starting transfers between devices: 6.29 us -> 7.93 us
  waiting for transfers between devices: 6.22 us -> 5.04 us
    all_gather x1 -> x0, blocking collectives: 5.79 us -> none  [on_device(): lax.all_gather(bc_local, 'head', axis=1, tiled=True).astype(jnp.float32)]
    dot_general x2, matrix products: 4.66 us -> 1.98 us  [block_pass(): carried = jnp.einsum('tn,hpn->htp', cmat, state, precision=high)]
    ppermute x0 -> x2, starting transfers between devices: none -> 1.63 us  [_process_boxes(): lax.ppermute(b_next, 'head', [(d, d ^ shaped) for d in range(odd)])]
    dot_general x2, matrix products: 1.85 us -> 0.36 us  [block_pass(): scores = jnp.dot(cmat, bmat.T, precision=high)]
    another operation x12, other arithmetic: 5.84 us -> 4.61 us
    ppermute x3, waiting for transfers between devices: 6.22 us -> 5.04 us  [shifted(): return lax.ppermute(value, axis, pairs)]
    exp x2, other arithmetic: 1.37 us -> 0.19 us  [block_pass(): jnp.exp(decay_t)[:, :, None] * carried]
    dot_general x2, matrix products: 2.81 us -> 3.85 us  [block_pass(): fresh = jnp.einsum('sh,shp,sn->hpn', to_end, values, bmat, precision=high)]
  transfers between devices with their start and end apart: 3 -> 5, of which waited for: 1 -> 1; matrix products, arithmetic and copies ran while one was open for 53% -> 64% of each run, Pallas kernels for 0% -> 0%
where the time goes in v1:
time: 84.3 us; the launch traced here: 83.6 us
  matrix products  28.9 us (34%)
  other arithmetic  21.6 us (26%)
  local copies, waits for them, and re-layouts  17.3 us (21%)
  starting transfers between devices  7.93 us (9%)
  waiting for transfers between devices  5.04 us (6%)
  between operations  2.85 us (3%)
    dot_general x2, matrix products, block_pass(): output = jnp.einsum('hts,shp->htp', weights, values, precision=high)  20.2 us
    ppermute x3, starting transfers between devices, shifted(): return lax.ppermute(value, axis, pairs)  6.3 us
    mul x1, local copies, waits for them, and re-layouts, gated_norm(): jax.nn.silu(gate.astype(jnp.float32)).reshape(rows, heads, width)  5.51 us
    slice x3, local copies, waits for them, and re-layouts, on_device(): block_values = x_conv[low:high_end].reshape(BLOCK, local_heads, HDIM)  5.47 us
    ppermute x3, waiting for transfers between devices, shifted(): return lax.ppermute(value, axis, pairs)  5.04 us
    mul x1, other arithmetic, gated_norm(): jax.nn.silu(gate.astype(jnp.float32)).reshape(rows, heads, width)  4.66 us
    another operation x12, other arithmetic  4.61 us
    mul x1, other arithmetic, causal_conv(): return jax.nn.silu(total)  4.2 us
  transfers between devices with their start and end apart: 5, of which 1 were waited for; matrix products, arithmetic and copies ran while one was open for 64% of the time, Pallas kernels for 0%

profile of v1, /device:TPU:0, one launch (start us, length us, event | category | flops | bytes accessed | tf_op | source)
XLA Modules:
  0.0 83.6 jit_solution(948416082036547305)
XLA Ops:
  0.0 1.0 %reduce-window.29 = s32[4,128]{1,0:T(4,128)S(1)} reduce-window(s32[4,128]{1,0:T(4,128)} %bitcast.140, s32[]{:T(128)} %constant.13.clone.1), window={size=1x128 pad=0_0x127_0}, to_apply=%region_0.0 | reduce-window | flops 65024 | bytes 4100 | tf_op jit(solution)/shard_map/reduce-window
  1.0 0.1 slice.151
  1.1 0.1 slice_reduce_fusion.5
  1.2 0.1 broadcast_compare_fusion
  1.3 0.6 fusion.84
  1.9 0.6 slice_compare_fusion
  2.5 1.0 %copy.44 = bf16[512,64]{1,0:T(8,128)(2,1)S(1)} copy(bf16[512,64]{0,1:T(8,128)(2,1)} %param.11) | data formatting | bytes 131072 | tf_op args[2]
  3.5 0.1 slice_select_fusion.1
  3.5 3.0 %collective-permute-start = (bf16[3,64]{1,0:T(4,128)(2,1)S(1)}, bf16[3,64]{1,0:T(4,128)(2,1)S(1)}, u32[]{:S(2)}, u32[]{:S(2)}) collective-permute-start(bf16[3,64]{1,0:T(4,128)(2,1)S(1)} %slice_select_fusion.1), channel_id=1, source_target_pairs={{0,4},{4,8},{8,12},{12,16},{16,20},{20,24},{24,28},{28,0},{1,5},{5... | collective-permute-start | bytes 1160 | tf_op jit(solution)/shard_map/ppermute | solution.py:27
  6.5 0.8 slice_select_fusion
  7.4 1.6 %collective-permute-start.3 = (bf16[3,2048]{1,0:T(4,128)(2,1)S(1)}, bf16[3,2048]{1,0:T(4,128)(2,1)S(1)}, u32[]{:S(2)}, u32[]{:S(2)}) collective-permute-start(bf16[3,2048]{1,0:T(4,128)(2,1)S(1)} %slice_select_fusion), channel_id=1, source_target_pairs={{0,4},{4,8},{8,12},{12,16},{16,20},{20,24},{24,28},{28,0},{1,5},{5... | collective-permute-start | bytes 36872 | tf_op jit(solution)/shard_map/ppermute | solution.py:27
  8.9 0.1 fusion.72
  9.0 0.7 slice.189
  9.7 0.6 slice.194
  10.3 0.1 fusion.50
  10.4 0.9 %multiply_bitcast_fusion.1 = (f32[4,2,8,128]{3,2,1,0:T(8,128)S(1)}, f32[4,2,8,128]{3,2,1,0:T(8,128)S(1)}) fusion(f32[512,32]{0,1:T(8,128)} %param.12, f32[32]{0:T(128)} %param.13), kind=kLoop, calls=%fused_computation.94 | loop fusion | flops 32768 | bytes 131200
  11.3 0.6 reduce-window.35
  11.9 0.2 slice_reduce_fusion.1
  12.1 0.1 fusion.82
  12.2 0.1 fusion.81
  12.8 0.9 %copy_bitcast_fusion = f32[32,4,128]{2,0,1:T(8,128)S(1)} fusion(f32[512,32]{0,1:T(8,128)} %param.12, f32[32]{0:T(128)} %param.13), kind=kLoop, calls=%fused_computation.65 | loop fusion | flops 32768 | bytes 131200 | tf_op jit(solution)/shard_map/reshape.13
  13.8 0.6 reduce-window.31
  14.3 0.2 slice_reduce_fusion.2
  14.5 0.1 copy_bitcast_fusion.2
  14.6 0.1 fusion.79
  14.7 1.2 %reduce-window.39 = f32[32,4,128]{2,0,1:T(8,128)S(1)} reduce-window(f32[32,4,128]{2,0,1:T(8,128)S(1)} %copy_bitcast_fusion, f32[]{:T(128)} %constant.14.clone.1), window={size=1x1x128 pad=0_0x0_0x127_0}, to_apply=%region_6.7 | reduce-window | flops 2080768 | bytes 131076 | tf_op jit(solution)/shard_map/reduce-window.6
  15.9 0.2 slice_reduce_fusion
  16.1 0.1 bitcast_bitcast_fusion
  16.2 0.1 bitcast_exponential_fusion
  16.3 0.8 bitcast_convert_fusion.3
  18.4 2.0 %broadcast_compare_fusion.1 = (pred[256]{0:T(512)(128)(4,1)S(1)}, pred[256]{0:T(512)(128)(4,1)S(1)}, pred[256]{0:T(512)(128)(4,1)S(1)}, pred[256]{0:T(512)(128)(4,1)S(1)}) fusion(s32[]{:T(128)} %bitcast.27, s32[4,128]{1,0:T(4,128)S(1)} %get-tuple-element.16, s32[]{:T(128)} %bitcast.19, s32[]{:T(128)} %bitcast.20), kind=kLoop, calls=%fused_computation.127 | loop fusion | flops 1024 | bytes 3084 | tf_op jit(solution)/shard_map/eq | solution.py:57
  20.4 0.2 slice_reduce_fusion.4
  20.6 0.9 %slice_convert_fusion.3 = (f32[1,2048]{1,0:T(1,128)S(1)}, f32[1,2048]{1,0:T(1,128)S(1)}, f32[1,2048]{1,0:T(1,128)S(1)}, f32[1,2048]{1,0:T(1,128)S(1)}) fusion(bf16[4,2048]{1,0:T(4,128)(2,1)} %param.14), kind=kLoop, calls=%fused_computation.107 | loop fusion | flops 8192 | bytes 49152 | tf_op jit(solution)/shard_map/mul | solution.py:34
  22.2 0.1 exponential_select_fusion.1
  22.3 0.2 slice_reduce_fusion.3
  22.4 0.1 exponential_select_fusion
  22.6 4.7 %convert_multiply_fusion = f32[512,2048]{1,0:T(8,128)} fusion(bf16[512,2048]{1,0:T(8,128)(2,1)} %param.10), kind=kLoop, calls=%fused_computation.12 | loop fusion | flops 5242880 | bytes 6291456 | tf_op jit(solution)/shard_map/jit(silu)/mul | solution.py:66
  27.2 0.2 fusion.71
  27.4 0.0 copy-start.3
  27.4 0.0 copy-start.2
  27.4 5.5 %copy.53 = f32[512,2048]{0,1:T(8,128)} copy(f32[512,2048]{1,0:T(8,128)} %convert_multiply_fusion) | data formatting | bytes 8388608 | tf_op jit(solution)/shard_map/jit(silu)/mul | solution.py:66
  33.0 0.1 reshape.296
  33.0 0.3 multiply_convert_fusion.1
  33.3 0.1 collective-permute-start.1
  33.4 4.2 %divide_multiply_fusion = f32[512,2048]{1,0:T(8,128)S(1)} fusion(bf16[512,2048]{1,0:T(8,128)(2,1)S(1)} %copy-done.2, bf16[3,2048]{1,0:T(4,128)(2,1)S(1)} %collective-permute-done.3, f32[2048]{0:T(1024)S(1)} %bitcast.138, f32[2048]{0:T(1024)S(1)} %bitcast.139, f32[2048]{0:T(1024)S(1)} %bitcast.137, f32[2048]{0:T(1024)S(1)} %bitcast.136, ...), kind=kLoop, calls=%fused_computation.25 | loop fusion | flops 28311552 | bytes 6338048 | tf_op jit(solution)/shard_map/jit(silu)/mul | solution.py:38
  37.6 0.1 maximum_select_fusion.1
  37.8 1.6 %collective-permute-start.2 = (bf16[512,128]{1,0:T(8,128)(2,1)S(1)}, bf16[512,128]{1,0:T(8,128)(2,1)S(1)}, u32[]{:S(2)}, u32[]{:S(2)}) collective-permute-start(bf16[512,128]{1,0:T(8,128)(2,1)S(1)} %maximum_select_fusion.1), channel_id=1, source_target_pairs={{0,2},{1,3},{2,0},{3,1},{4,6},{5,7},{6,4},{7,5},{8,10},{9,11},{10,... | collective-permute-start | bytes 393224 | tf_op jit(solution)/shard_map/ppermute | solution.py:16
  39.4 1.7 %fusion.83 = (f32[256,2048]{1,0:T(8,128)}, f32[256,2048]{1,0:T(8,128)S(1)}) fusion(f32[512,2048]{1,0:T(8,128)S(1)} %divide_multiply_fusion), kind=kLoop, calls=%fused_computation.139 | loop fusion | bytes 8388608 | tf_op jit(solution)/shard_map/slice | solution.py:99
  41.1 1.9 %copy.47 = f32[256,2048]{0,1:T(8,128)} copy(f32[256,2048]{1,0:T(8,128)S(1)} %get-tuple-element.20) | data formatting | bytes 4194304 | tf_op jit(solution)/shard_map/slice | solution.py:99
  42.9 1.9 %copy.50 = f32[256,2048]{0,1:T(8,128)S(1)} copy(f32[256,2048]{1,0:T(8,128)} %get-tuple-element.18) | data formatting | bytes 4194304 | tf_op jit(solution)/shard_map/slice | solution.py:99
  44.9 0.1 maximum_select_fusion
  44.9 0.2 fusion.60
  45.1 2.7 %fusion.37 = f32[32,64,128]{2,1,0:T(8,128)S(1)} fusion(f32[256,32,64]{0,2,1:T(8,128)} %bitcast.131, f32[256,32]{0,1:T(8,128)S(1)} %exponential_select_fusion.1, f32[32]{0:T(128)S(1)} %fusion.75, bf16[512,256]{1,0:T(8,128)(2,1)S(1)} %maximum_select_fusion), kind=kOutput, calls=%fused_computation.44 | convolution fusion | flops 806092800 | bytes 3244544 | tf_op jit(solution)/shard_map/sh,shp,sn->hpn/dot_general | solution.py:59
  47.8 1.0 %fusion.55 = f32[32,64,256]{2,1,0:T(8,128)S(1)} fusion(f32[32,64,128]{2,1,0:T(8,128)S(1)} %fusion.37, bf16[512,256]{1,0:T(8,128)(2,1)S(1)} %maximum_select_fusion), kind=kOutput, calls=%fused_computation.68 | convolution fusion | flops 805306368 | bytes 3211264 | tf_op jit(solution)/shard_map/tn,hpn->htp/dot_general | solution.py:55
  48.9 1.1 %fusion.43 = f32[32,64,128]{2,1,0:T(8,128)S(1)} fusion(f32[256,32,64]{0,2,1:T(8,128)S(1)} %bitcast.129, f32[256,32]{0,1:T(8,128)S(1)} %exponential_select_fusion, f32[32,64,128]{2,1,0:T(8,128)S(1)} %fusion.37, f32[32]{0:T(128)S(1)} %broadcast_select_fusion, f32[32]{0:T(128)S(1)} %fusion.71, bf16[512,256]{1,0:T(8,128)(2,1)S(1)} %maximum_select_fusion), kind=kOutput, calls=%fused_computation.46 | convolution fusion | flops 806617088 | bytes 4293632 | tf_op jit(solution)/shard_map/sh,shp,sn->hpn/dot_general | solution.py:59
  50.0 1.8 %collective-permute-start.4 = (f32[32,64,128]{2,1,0:T(8,128)S(1)}, f32[32,64,128]{2,1,0:T(8,128)S(1)}, u32[]{:S(2)}, u32[]{:S(2)}) collective-permute-start(f32[32,64,128]{2,1,0:T(8,128)S(1)} %fusion.43), channel_id=1, source_target_pairs={{0,4},{4,8},{8,12},{12,16},{16,20},{20,24},{24,28},{28,0},{1,5},{5... | collective-permute-start | bytes 3145736 | tf_op jit(solution)/shard_map/while/body/eval_jaxpr/ppermute | solution.py:27
  51.8 10.0 %bitcast_add_fusion = f32[32,256,64]{1,2,0:T(8,128)S(1)} fusion(f32[32,64,256]{2,1,0:T(8,128)S(1)} %fusion.55, f32[256,32,64]{0,2,1:T(8,128)S(1)} %bitcast.130, f32[256,256]{1,0:T(8,128)S(1)} %fusion.60, f32[32,256]{1,0:T(8,128)S(1)} %get-tuple-element.24, pred[256,256]{1,0:T(8,128)(4,1)S(1)} %get-tuple-element.50, f32[32,256]{1,0:T(8,128)S(1)} %fusion.81, ...), kind=kOutput, calls=%fused_computation.38 | convolution fusion | flops 1620574208 | bytes 6684928 | tf_op jit(solution)/shard_map/hts,shp->htp/dot_general | solution.py:53
  61.7 0.2 fusion.65
  61.9 1.0 %fusion.48 = f32[32,64,256]{2,1,0:T(8,128)S(1)} fusion(bf16[512,256]{1,0:T(8,128)(2,1)S(1)} %maximum_select_fusion), kind=kOutput, calls=%fused_computation.49 | convolution fusion | flops 805306368 | bytes 2162688 | tf_op jit(solution)/shard_map/tn,hpn->htp/dot_general | solution.py:55
  62.9 10.2 %bitcast_add_fusion.1 = f32[32,256,64]{1,2,0:T(8,128)S(1)} fusion(f32[32,64,256]{2,1,0:T(8,128)S(1)} %fusion.48, f32[256,32,64]{0,2,1:T(8,128)S(1)} %bitcast.132, f32[256,256]{1,0:T(8,128)S(1)} %fusion.65, f32[32,256]{1,0:T(8,128)S(1)} %get-tuple-element.25, pred[256,256]{1,0:T(8,128)(4,1)S(1)} %get-tuple-element.51, f32[32,256]{1,0:T(8,128)S(1)} %fusion.79, ...), kind=kOutput, calls=%fused_computation.39 | convolution fusion | flops 1620574208 | bytes 6684928 | tf_op jit(solution)/shard_map/hts,shp->htp/dot_general | solution.py:53
  73.1 5.0 %collective-permute-done.4 = f32[32,64,128]{2,1,0:T(8,128)S(1)} collective-permute-done((f32[32,64,128]{2,1,0:T(8,128)S(1)}, f32[32,64,128]{2,1,0:T(8,128)S(1)}, u32[]{:S(2)}, u32[]{:S(2)}) %collective-permute-start.4) | collective-permute-done | bytes 1048608 | tf_op jit(solution)/shard_map/while/body/eval_jaxpr/ppermute | solution.py:27
  78.2 2.5 %multiply_reduce_fusion = (f32[512,32]{0,1:T(8,128)S(1)}, f32[512,32,64]{0,2,1:T(8,128)S(1)}) fusion(f32[512,32,64]{0,2,1:T(8,128)S(1)} %bitcast.127, f32[32,64,128]{2,1,0:T(8,128)S(1)} %collective-permute-done.4, bf16[512,256]{1,0:T(8,128)(2,1)S(1)} %maximum_select_fusion, f32[32,512]{1,0:T(8,128)S(1)} %bitcast_exponential_fusion, ...), kind=kOutput, calls=%fused_computation.21 | convolution fusion | flops 1617936384 | bytes 13894144 | tf_op jit(solution)/shard_map/tn,hpn->htp/dot_general | solution.py:119
  80.7 0.5 multiply_convert_fusion
  81.3 2.4 %copy.54 = bf16[512,2048]{1,0:T(8,128)(2,1)} copy(bf16[512,2048]{0,1:T(8,128)(2,1)S(1)} %bitcast.128) | data formatting | bytes 4194304 | tf_op jit(solution)/shard_map/convert_element_type | solution.py:69
  (22 shorter events, 0.2 us)
Async XLA Ops:
  3.5 29.5 %collective-permute-start = (bf16[3,64]{1,0:T(4,128)(2,1)S(1)}, bf16[3,64]{1,0:T(4,128)(2,1)S(1)}, u32[]{:S(2)}, u32[]{:S(2)}) collective-permute-start(bf16[3,64]{1,0:T(4,128)(2,1)S(1)} %slice_select_fusion.1), channel_id=1, source_target_pairs={{0,4},{4,8},{8,12},{12,16},{16,20},{20,24},{24,28},{28,0},{1,5},{5... | collective-permute-start | bytes 1160 | tf_op jit(solution)/shard_map/ppermute | solution.py:27
  7.4 26.1 %collective-permute-start.3 = (bf16[3,2048]{1,0:T(4,128)(2,1)S(1)}, bf16[3,2048]{1,0:T(4,128)(2,1)S(1)}, u32[]{:S(2)}, u32[]{:S(2)}) collective-permute-start(bf16[3,2048]{1,0:T(4,128)(2,1)S(1)} %slice_select_fusion), channel_id=1, source_target_pairs={{0,4},{4,8},{8,12},{12,16},{16,20},{20,24},{24,28},{28,0},{1,5},{5... | collective-permute-start | bytes 36872 | tf_op jit(solution)/shard_map/ppermute | solution.py:27
  27.4 5.5 %copy-start.3 = (bf16[2048]{0:T(1024)(128)(2,1)S(1)}, bf16[2048]{0:T(1024)(128)(2,1)}, u32[]{:S(2)}) copy-start(bf16[2048]{0:T(1024)(128)(2,1)} %param.16) | copy-start | bytes 12292
  27.4 6.0 %copy-start.2 = (bf16[512,2048]{1,0:T(8,128)(2,1)S(1)}, bf16[512,2048]{1,0:T(8,128)(2,1)}, u32[]{:S(2)}) copy-start(bf16[512,2048]{1,0:T(8,128)(2,1)} %param.9) | copy-start | bytes 6291460
  33.3 4.3 %collective-permute-start.1 = (bf16[512,64]{1,0:T(8,128)(2,1)S(1)}, bf16[512,64]{1,0:T(8,128)(2,1)S(1)}, u32[]{:S(2)}, u32[]{:S(2)}) collective-permute-start(bf16[512,64]{1,0:T(8,128)(2,1)S(1)} %multiply_convert_fusion.1), channel_id=1, source_target_pairs={{0,1},{1,0},{2,3},{3,2},{4,5},{5,4},{6,7},{7,6},{8,9},{9,8},{10,11... | collective-permute-start | bytes 196616 | tf_op jit(solution)/shard_map/ppermute | solution.py:16
  37.8 7.0 %collective-permute-start.2 = (bf16[512,128]{1,0:T(8,128)(2,1)S(1)}, bf16[512,128]{1,0:T(8,128)(2,1)S(1)}, u32[]{:S(2)}, u32[]{:S(2)}) collective-permute-start(bf16[512,128]{1,0:T(8,128)(2,1)S(1)} %maximum_select_fusion.1), channel_id=1, source_target_pairs={{0,2},{1,3},{2,0},{3,1},{4,6},{5,7},{6,4},{7,5},{8,10},{9,11},{10,... | collective-permute-start | bytes 393224 | tf_op jit(solution)/shard_map/ppermute | solution.py:16
  50.0 28.2 %collective-permute-start.4 = (f32[32,64,128]{2,1,0:T(8,128)S(1)}, f32[32,64,128]{2,1,0:T(8,128)S(1)}, u32[]{:S(2)}, u32[]{:S(2)}) collective-permute-start(f32[32,64,128]{2,1,0:T(8,128)S(1)} %fusion.43), channel_id=1, source_target_pairs={{0,4},{4,8},{8,12},{12,16},{16,20},{20,24},{24,28},{28,0},{1,5},{5... | collective-permute-start | bytes 3145736 | tf_op jit(solution)/shard_map/while/body/eval_jaxpr/ppermute | solution.py:27
  51.8 11.1 %copy-start.1 = (f32[256,2048]{0,1:T(8,128)S(1)}, f32[256,2048]{0,1:T(8,128)}, u32[]{:S(2)}) copy-start(f32[256,2048]{0,1:T(8,128)} %copy.47) | copy-start | bytes 6291460
  62.9 15.3 %copy-start = (f32[512,2048]{0,1:T(8,128)S(1)}, f32[512,2048]{0,1:T(8,128)}, u32[]{:S(2)}) copy-start(f32[512,2048]{0,1:T(8,128)} %copy.53) | copy-start | bytes 12582916
